TPU v7x, 32 devices: a whole 2x2x4 slice. The times are simulated.
32 devices in a mesh: epoch: 4 (over y, x), sky: 8 (over z, core).
Axes of the slice: x: 2, y: 2, z: 4, core: 2. Of those that a mesh axis runs over, the one named last changes fastest.
Arguments:
- image: bfloat16 [16, 384, 2048], P('epoch', 'sky'), may hold values from -400 to 400
- inv_variance: bfloat16 [16, 384, 2048], P('epoch', 'sky'), may hold values from 0.25 to 4
- psf_rows: float32 [9], replicated, may hold values from 0.05 to 1
- psf_cols: float32 [9], replicated, may hold values from 0.05 to 1
- shift_num: int32 [4, 16], replicated, may hold values from -64 to 64, as said below
Outputs:
- search_map: float32 [384, 2048], P('sky', 'epoch')
Inputs may be any that keep to these rules, and one draw needn't show every extreme that they name: `shift_num`: at level l every entry has magnitude at most 4 * 2 * 2^l, and at each level some entry equals plus and some other entry minus that bound.
All inputs are finite; a program needn't handle non-finite values.
Results may differ from a plain program's by a relative error of at most 0.0024.
Values may be sent and summed in bfloat16 or wider, within the bound.
A program may use at most 64 MiB of HBM per device.

v0:
```python
import functools

import jax
import jax.numpy as jnp
from jax import lax
from jax.experimental import pallas as pl
from jax.experimental.pallas import tpu as pltpu
from jax.sharding import PartitionSpec as P

LEVELS = 4
PSF_HALF = 4
DEN = 4
VMAX = 2
LANES = 128
SUB = 8
BSUB = 16
MESH = pl.DeviceIdType.MESH


def flip(index, mask, size):
    result, bit = 0, 1
    while bit < size:
        digit = lax.rem(lax.div(index, bit), 2)
        result = result + bit * ((1 - digit) if mask & bit else digit)
        bit *= 2
    return result


def up_to(value, step):
    return (value + step - 1) // step


LAG = 3
PAIRS = 2
STEP = 16


def SEND_ORDER(n):
    return list(range(1, n)) + [0]


def kernel(
    n, sky, image, variance, psf_rows, psf_cols, shift_num, out,
    outgoing, pieces, above, below, bands, rows_in, *rest,
):
    send_sem, recv_sem, down_send, down_recv, up_send, up_recv = rest[-6:]
    stacks = rest[:-6]
    ep_local, row_count = image.shape[0], image.shape[1]
    epochs = n * ep_local
    tiles = image.shape[2] // n // LANES
    blocks = row_count // SUB
    reach = PSF_HALF
    local_levels = ep_local.bit_length() - 1
    me = lax.axis_index("epoch")
    row_dev = lax.axis_index("sky")
    has_above = row_dev > 0
    has_below = row_dev < sky - 1
    groups = [flip(me, d, n) for d in range(n)]

    barrier = pltpu.get_barrier_semaphore()
    for d in range(1, n):
        pl.semaphore_signal(barrier, inc=1, device_id=(groups[d], row_dev), device_id_type=MESH)

    @pl.when(has_above)
    def _():
        pl.semaphore_signal(barrier, inc=1, device_id=(me, row_dev - 1), device_id_type=MESH)

    @pl.when(has_below)
    def _():
        pl.semaphore_signal(barrier, inc=1, device_id=(me, row_dev + 1), device_id_type=MESH)

    def make_bands():
        source = lax.broadcasted_iota(jnp.int32, (2 * LANES, LANES), 0)
        column = lax.broadcasted_iota(jnp.int32, (2 * LANES, LANES), 1)
        at = jnp.where(source < LANES + LANES // 2, source, source - 2 * LANES)
        tap = at - column + reach
        for m in range(2):
            band = jnp.zeros((2 * LANES, LANES), jnp.float32)
            for b in range(2 * reach + 1):
                weight = psf_cols[b] if m == 0 else psf_cols[b] * psf_cols[b]
                band = jnp.where(tap == b, weight, band)
            high = band.astype(jnp.bfloat16)
            bands[m, :, :LANES] = high
            bands[m, :, LANES:] = (band - high.astype(jnp.float32)).astype(jnp.bfloat16)

    lane = lax.broadcasted_iota(jnp.int32, (ep_local * row_count, LANES), 1)

    def filter_cols(p, tile, dest):
        here = p * tiles + tile
        flat = (ep_local * row_count, LANES)

        def take(ref, t):
            at = pl.multiple_of(t * LANES, LANES)
            return ref[:, :, pl.ds(at, LANES)].astype(jnp.float32).reshape(flat)

        def both(t, keep):
            v = take(variance, t)
            if keep is not None:
                v = v * keep
            return take(image, t) * v, v

        total = n * tiles
        left_on = jnp.where(here > 0, 1.0, 0.0).astype(jnp.float32)
        right_on = jnp.where(here < total - 1, 1.0, 0.0).astype(jnp.float32)
        left = both(jnp.maximum(here - 1, 0), left_on)
        centre = both(here, None)
        right = both(jnp.minimum(here + 1, total - 1), right_on)
        for m in range(2):
            edge = jnp.where(lane < LANES // 2, right[m], left[m])
            x = jnp.concatenate([centre[m], edge], axis=1)
            high = x.astype(jnp.bfloat16)
            y = jnp.dot(high, bands[m], preferred_element_type=jnp.float32)
            y = y[:, :LANES] + y[:, LANES:]
            if m == 0:
                low = (x - high.astype(jnp.float32)).astype(jnp.bfloat16)
                y = y + jnp.dot(low, bands[m, :, :LANES], preferred_element_type=jnp.float32)
            dest[:, m] = y.reshape(ep_local, row_count, LANES).astype(jnp.bfloat16)

    def piece_copy(d, tile):
        return pltpu.make_async_remote_copy(
            src_ref=outgoing.at[d - 1, tile], dst_ref=pieces.at[d, tile],
            send_sem=send_sem.at[d, tile], recv_sem=recv_sem.at[d, tile],
            device_id=(groups[d], row_dev), device_id_type=MESH,
        )

    def halo_rows(g):
        last = (g + 1) * ep_local - 1
        return BSUB * up_to(SUB * up_to(VMAX * last, SUB) + reach, BSUB)

    def to_below(d, tile, g):
        h = halo_rows(g)
        rows = pl.ds(row_count - h, h)
        return pltpu.make_async_remote_copy(
            src_ref=pieces.at[d, tile, :, :, rows, :], dst_ref=above.at[d, tile, :, :, rows, :],
            send_sem=down_send.at[d, tile], recv_sem=down_recv.at[d, tile],
            device_id=(me, row_dev + 1), device_id_type=MESH,
        )

    def to_above(d, tile, g):
        rows = pl.ds(0, halo_rows(g))
        return pltpu.make_async_remote_copy(
            src_ref=pieces.at[d, tile, :, :, rows, :], dst_ref=below.at[d, tile, :, :, rows, :],
            send_sem=up_send.at[d, tile], recv_sem=up_recv.at[d, tile],
            device_id=(me, row_dev - 1), device_id_type=MESH,
        )

    def each_group(d, use):
        for g in range(n):
            pl.when(groups[d] == g)(functools.partial(use, g))

    def forward(d, tile):
        def use(g):
            @pl.when(has_below)
            def _():
                to_below(d, tile, g).start()

            @pl.when(has_above)
            def _():
                to_above(d, tile, g).start()

        each_group(d, use)

    def wait_halo(d, tile):
        def use(g):
            @pl.when(has_above)
            def _():
                to_below(d, tile, g).wait_recv()

            @pl.when(has_below)
            def _():
                to_above(d, tile, g).wait_recv()

        each_group(d, use)

    def wait_sent(d, tile):
        def use(g):
            @pl.when(has_below)
            def _():
                to_below(d, tile, g).wait_send()

            @pl.when(has_above)
            def _():
                to_above(d, tile, g).wait_send()

        each_group(d, use)

    def bounds(pad):
        low = jnp.where(has_above, -pad, 0)
        high = jnp.where(has_below, row_count // STEP + pad, row_count // STEP)
        return low, high

    def row_at(block, step=STEP):
        return pl.multiple_of(row_count + block * step, step)

    def unpack(d, tile, g):
        last = (g + 1) * ep_local - 1
        count = up_to(SUB * up_to(VMAX * last, SUB) + reach, BSUB)
        per = row_count // BSUB

        def rows_of(source, part, low, high):
            def body(i, carry):
                r = pl.multiple_of(i * BSUB, BSUB)
                to = pl.multiple_of(part * row_count + i * BSUB, BSUB)
                for e in range(ep_local):
                    for m in range(2):
                        rows_in[e, m, pl.ds(to, BSUB), :] = source[
                            d, tile, e, m, pl.ds(r, BSUB), :
                        ].astype(jnp.float32)
                return carry

            lax.fori_loop(low, high, body, 0)

        rows_of(above, 0, jnp.where(has_above, per - count, per), per)
        rows_of(pieces, 1, 0, per)
        rows_of(below, 2, 0, jnp.where(has_below, count, 0))

    def filter_rows(g, dest):
        w = [psf_rows[b] for b in range(2 * reach + 1)]
        squares = [s * s for s in w]
        low, high = bounds(up_to(VMAX * ((g + 1) * ep_local - 1), STEP))

        def body(b, carry):
            at = row_at(b)
            totals = {}
            for e in range(ep_local):
                for m in range(2):
                    weights = w if m == 0 else squares
                    parts = [
                        weights[a] * rows_in[e, m, pl.ds(at + (a - reach), STEP), :]
                        for a in range(2 * reach + 1)
                    ]
                    totals[e, m] = functools.reduce(jnp.add, parts)
            for (e, m), total in totals.items():
                dest[e, m, pl.ds(at, STEP), :] = total
            return carry

        lax.fori_loop(low, high, body, 0)

    def shift_of(level, index):
        number = shift_num[level, index]
        big = 2 * VMAX * 2**LEVELS
        whole = lax.div(number + DEN * big, DEN) - big
        left = number - whole * DEN
        fraction = left.astype(jnp.float32) / DEN
        return whole, whole + jnp.where(left > 0, 1, 0), fraction

    def level_pass(level, src, dest, base, pairs, pad, dest_base):
        half = 2**level
        moves = [
            (j, [(i, shift_of(level, base + i)) for i in (j, j + half)]) for j in pairs
        ]
        low, high = bounds(pad)

        def body(b, carry):
            at = row_at(b)
            for some in range(0, len(moves), PAIRS):
                results = []
                for j, outs in moves[some:some + PAIRS]:
                    for m in range(2):
                        lower = src[j, m, pl.ds(at, STEP), :]
                        for index, (near, far, fraction) in outs:
                            x = src[j + half, m, pl.ds(at - near, STEP), :]
                            y = src[j + half, m, pl.ds(at - far, STEP), :]
                            mixed = (1.0 - fraction) * x + fraction * y
                            results.append((index, m, lower + mixed))
                for index, m, result in results:
                    dest[dest_base + index, m, pl.ds(at, STEP), :] = result
            return carry

        lax.fori_loop(low, high, body, 0)

    local, wide = stacks[:local_levels], stacks[local_levels:]

    def process(d, tile):
        g = groups[d]
        wait_halo(d, tile)
        unpack(d, tile, g)
        filter_rows(g, local[0])
        for level in range(local_levels):
            last = level == local_levels - 1
            half = 2**level
            pairs = [j for j in range(ep_local) if not j & half]
            top = g * ep_local + ep_local - 2 * half
            level_pass(
                level, local[level], wide[0] if last else local[level + 1],
                g * ep_local, pairs, up_to(VMAX * top, STEP), g * ep_local if last else 0,
            )

    def finish(tile):
        for level in range(local_levels, LEVELS - 1):
            half = 2**level
            for first in range(0, epochs, 2 * half):
                level_pass(
                    level, wide[level - local_levels], wide[level - local_levels + 1], 0,
                    list(range(first, first + half)), up_to(VMAX * first, STEP), 0,
                )
        final = wide[LEVELS - 1 - local_levels]
        half = epochs // 2

        def body(b, carry):
            at = row_at(b, SUB)
            likelihood = [None] * epochs
            for j in range(half):
                lower = [final[j, m, pl.ds(at, SUB), :] for m in range(2)]
                for index in (j, j + half):
                    near, far, fraction = shift_of(LEVELS - 1, index)
                    maps = []
                    for m in range(2):
                        x = final[j + half, m, pl.ds(at - near, SUB), :]
                        y = final[j + half, m, pl.ds(at - far, SUB), :]
                        maps.append(lower[m] + ((1.0 - fraction) * x + fraction * y))
                    likelihood[index] = maps[0] * lax.rsqrt(maps[1])
            peak = functools.reduce(jnp.maximum, likelihood)
            total = functools.reduce(jnp.add, [jnp.exp(x - peak) for x in likelihood])
            to = pl.multiple_of(b * SUB, SUB)
            out[pl.ds(to, SUB), tile * LANES:(tile + 1) * LANES] = peak + jnp.log(total)
            return carry

        lax.fori_loop(0, blocks, body, 0)

    make_bands()
    for tile in range(tiles):
        for d in SEND_ORDER(n):
            filter_cols(groups[d], tile, outgoing.at[d - 1, tile] if d else pieces.at[0, tile])
            if tile == 0 and d == SEND_ORDER(n)[0]:
                near = jnp.where(has_above, 1, 0) + jnp.where(has_below, 1, 0)
                pl.semaphore_wait(barrier, n - 1 + near)
            if d:
                piece_copy(d, tile).start()
            else:
                forward(0, tile)

    for edge, part in ((has_above, 0), (has_below, 2)):
        @pl.when(jnp.logical_not(edge))
        def _():
            for ref in (rows_in,) + stacks:
                zero = jnp.zeros((row_count, LANES), jnp.float32)

                def body(e, carry):
                    for m in range(2):
                        ref[e, m, pl.ds(part * row_count, row_count), :] = zero
                    return carry

                lax.fori_loop(0, ref.shape[0], body, 0)

    steps = [(tile, d) for tile in range(tiles) for d in range(n)]
    for i in range(len(steps) + LAG):
        if i < len(steps):
            tile, d = steps[i]
            if d:
                piece_copy(d, tile).wait_recv()
                forward(d, tile)
        if i >= LAG:
            tile, d = steps[i - LAG]
            process(d, tile)
            if d == n - 1:
                finish(tile)

    for tile, d in steps:
        if d:
            piece_copy(d, tile).wait_send()
        wait_sent(d, tile)


def on_device(n, sky, image, inv_variance, psf_rows, psf_cols, shift_num):
    ep_local, row_count, cols = image.shape
    tiles = cols // n // LANES
    local_levels = ep_local.bit_length() - 1
    piece = (tiles, ep_local, 2, row_count, LANES)

    def tall(count):
        return pltpu.VMEM((count, 2, 3 * row_count, LANES), jnp.float32)

    vmem = pl.BlockSpec(memory_space=pltpu.VMEM)
    smem = pl.BlockSpec(memory_space=pltpu.SMEM)
    return pl.pallas_call(
        functools.partial(kernel, n, sky),
        out_shape=jax.ShapeDtypeStruct((row_count, cols // n), jnp.float32),
        in_specs=[vmem, vmem, smem, smem, smem],
        out_specs=vmem,
        scratch_shapes=[
            pltpu.VMEM((n - 1,) + piece, jnp.bfloat16),
            pltpu.VMEM((n,) + piece, jnp.bfloat16),
            pltpu.VMEM((n,) + piece, jnp.bfloat16),
            pltpu.VMEM((n,) + piece, jnp.bfloat16),
            pltpu.VMEM((2, 2 * LANES, 2 * LANES), jnp.bfloat16),
            tall(ep_local),
        ]
        + [tall(ep_local) for _ in range(local_levels)]
        + [tall(n * ep_local) for _ in range(LEVELS - local_levels)]
        + [pltpu.SemaphoreType.DMA((n, tiles)) for _ in range(6)],
        compiler_params=pltpu.CompilerParams(
            collective_id=0, has_side_effects=True, vmem_limit_bytes=60 * 1024 * 1024
        ),
    )(image, inv_variance, psf_rows, psf_cols, shift_num)


def solution(mesh):
    body = functools.partial(on_device, mesh.shape["epoch"], mesh.shape["sky"])
    return jax.shard_map(
        body,
        mesh=mesh,
        in_specs=(P("epoch", "sky", None), P("epoch", "sky", None), P(), P(), P()),
        out_specs=P("sky", "epoch"),
        check_vma=False,
    )
```

profile of v0, /device:TPU:1, one launch (start us, length us, event | category | flops | bytes accessed | tf_op | source)
XLA Modules:
  0.0 36.8 jit_solution(11361441091457076342)
XLA Ops:
  0.0 35.3 %shard_map.55 = f32[48,512]{1,0:T(8,128)} custom-call(bf16[4,48,2048]{2,1,0:T(8,128)(2,1)} %image.1, bf16[4,48,2048]{2,1,0:T(8,128)(2,1)} %variance.1, f32[9]{0:T(128)} %psf_rows.1, f32[9]{0:T(128)} %psf_cols.1, s32[4,16]{1,0:T(4,128)} %shift_num.1), custom_call_target="tpu_custom_call" | custom-call | tf_op jit(solution)/shard_map/pallas_call | solution.py:376
  35.3 1.5 %copy.7 = f32[48,512]{1,0:T(8,128)} copy(f32[48,512]{1,0:T(8,128)} %shard_map.55) | data formatting | bytes 196608
where the time goes:
time: 37 us; the launch traced here: 36.8 us
  Pallas kernels  35.3 us (95%)
  local copies, waits for them, and re-layouts  1.54 us (4%)
    pallas_call x1, Pallas kernels, on_device(): pl.pallas_call(functools.partial(kernel, n, sky), out_shape=jax.ShapeDtyp...  35.3 us
    unnamed x1, local copies, waits for them, and re-layouts  1.54 us

commit v1 on v0

v1 whole, which is shorter than its diff:
```python
import functools

import jax
import jax.numpy as jnp
from jax import lax
from jax.experimental import pallas as pl
from jax.experimental.pallas import tpu as pltpu
from jax.sharding import PartitionSpec as P

LEVELS = 4
PSF_HALF = 4
DEN = 4
VMAX = 2
LANES = 128
SUB = 8
BSUB = 16
MESH = pl.DeviceIdType.MESH


def flip(index, mask, size):
    result, bit = 0, 1
    while bit < size:
        digit = lax.rem(lax.div(index, bit), 2)
        result = result + bit * ((1 - digit) if mask & bit else digit)
        bit *= 2
    return result


def round_up(value, step):
    return (value + step - 1) // step * step


def halo_of(epoch):
    return round_up(VMAX * epoch + PSF_HALF, BSUB)


def classes_of(epochs):
    found = {}
    for e in range(epochs):
        first, count = found.get(halo_of(e), (e, 0))
        found[halo_of(e)] = (first, count + 1)
    return found


def runs_of(g, ep_local):
    runs = []
    for e in range(g * ep_local, (g + 1) * ep_local):
        if runs and runs[-1][0] == halo_of(e):
            runs[-1] = (runs[-1][0], runs[-1][1], runs[-1][2] + 1)
        else:
            runs.append((halo_of(e), e, 1))
    return runs


def plan_of(g, ep_local, row_count):
    blocks, used, left = [], [], []
    for e in range(ep_local):
        h = halo_of(g * ep_local + e)
        size = row_count + 2 * h
        first = min(size, LANES)
        blocks.append((e, len(used), 0, -h, first))
        used.append(first)
        if size > first:
            left.append((e, first - h, size - first))
    for e, row, size in left:
        at = next((t for t, u in enumerate(used) if u + size <= LANES), None)
        if at is None:
            at = len(used)
            used.append(0)
        blocks.append((e, at, used[at], row, size))
        used[at] += size
    return blocks, used


SEND_ORDER = "3120"


def send_order(n):
    if n == len(SEND_ORDER):
        return [int(c) for c in SEND_ORDER]
    return list(range(n - 1, 0, -1)) + [0]


def kernel(
    n, sky, image_hbm, variance_hbm, psf_rows, psf_cols, shift_num, out,
    image, variance, outgoing, pieces, bands, toeplitz, mid, *rest,
):
    ep_local, row_count = image.shape[0], image.shape[1]
    epochs = n * ep_local
    tiles = image.shape[2] // n // LANES
    reach = PSF_HALF
    local_levels = ep_local.bit_length() - 1
    classes = classes_of(epochs)
    runs = [runs_of(g, ep_local) for g in range(n)]
    plans = [plan_of(g, ep_local, row_count) for g in range(n)]
    rest = list(rest)
    above = {h: rest.pop(0) for h in classes}
    below = {h: rest.pop(0) for h in classes}
    matrices = [rest.pop(0) for _ in range(n)]
    wide = [rest.pop(0) for _ in range(LEVELS - local_levels)]
    in_sem, send_sem, recv_sem, down_send, down_recv, up_send, up_recv = rest
    class_at = {h: i for i, h in enumerate(classes)}
    run_at = {}
    for g in range(n):
        for run in runs[g]:
            run_at[run] = len(run_at)

    me = lax.axis_index("epoch")
    row_dev = lax.axis_index("sky")
    has_above = row_dev > 0
    has_below = row_dev < sky - 1
    groups = [flip(me, d, n) for d in range(n)]

    loads = [
        pltpu.make_async_copy(image_hbm, image, in_sem.at[0]),
        pltpu.make_async_copy(variance_hbm, variance, in_sem.at[1]),
    ]
    for load in loads:
        load.start()

    barrier = pltpu.get_barrier_semaphore()
    for d in range(1, n):
        pl.semaphore_signal(barrier, inc=1, device_id=(groups[d], row_dev), device_id_type=MESH)

    @pl.when(has_above)
    def _():
        pl.semaphore_signal(barrier, inc=1, device_id=(me, row_dev - 1), device_id_type=MESH)

    @pl.when(has_below)
    def _():
        pl.semaphore_signal(barrier, inc=1, device_id=(me, row_dev + 1), device_id_type=MESH)

    def make_bands():
        source = lax.broadcasted_iota(jnp.int32, (2 * LANES, LANES), 0)
        column = lax.broadcasted_iota(jnp.int32, (2 * LANES, LANES), 1)
        at = jnp.where(source < LANES + LANES // 2, source, source - 2 * LANES)
        tap = at - column + reach
        for m in range(2):
            band = jnp.zeros((2 * LANES, LANES), jnp.float32)
            for b in range(2 * reach + 1):
                weight = psf_cols[b] if m == 0 else psf_cols[b] * psf_cols[b]
                band = jnp.where(tap == b, weight, band)
            high = band.astype(jnp.bfloat16)
            bands[m, :, :LANES] = high
            bands[m, :, LANES:] = (band - high.astype(jnp.float32)).astype(jnp.bfloat16)

    lane = lax.broadcasted_iota(jnp.int32, (ep_local * row_count, LANES), 1)

    def filter_cols(p, tile, dest):
        here = p * tiles + tile
        flat = (ep_local * row_count, LANES)

        def take(ref, t):
            at = pl.multiple_of(t * LANES, LANES)
            return ref[:, :, pl.ds(at, LANES)].astype(jnp.float32).reshape(flat)

        def both(t, keep):
            v = take(variance, t)
            if keep is not None:
                v = v * keep
            return take(image, t) * v, v

        total = n * tiles
        left_on = jnp.where(here > 0, 1.0, 0.0).astype(jnp.float32)
        right_on = jnp.where(here < total - 1, 1.0, 0.0).astype(jnp.float32)
        left = both(jnp.maximum(here - 1, 0), left_on)
        centre = both(here, None)
        right = both(jnp.minimum(here + 1, total - 1), right_on)
        for m in range(2):
            edge = jnp.where(lane < LANES // 2, right[m], left[m])
            x = jnp.concatenate([centre[m], edge], axis=1)
            high = x.astype(jnp.bfloat16)
            y = jnp.dot(high, bands[m], preferred_element_type=jnp.float32)
            y = y[:, :LANES] + y[:, LANES:]
            if m == 0:
                low = (x - high.astype(jnp.float32)).astype(jnp.bfloat16)
                y = y + jnp.dot(low, bands[m, :, :LANES], preferred_element_type=jnp.float32)
            dest[:, m] = y.reshape(ep_local, row_count, LANES).astype(jnp.bfloat16)

    def piece_out(d, tile):
        return pltpu.make_async_remote_copy(
            src_ref=outgoing.at[d - 1, tile], dst_ref=pieces.at[me, tile],
            send_sem=send_sem.at[0], recv_sem=recv_sem.at[me, tile],
            device_id=(groups[d], row_dev), device_id_type=MESH,
        )

    def piece_in(d, tile):
        return pltpu.make_async_remote_copy(
            src_ref=outgoing.at[d - 1, tile], dst_ref=pieces.at[groups[d], tile],
            send_sem=send_sem.at[0], recv_sem=recv_sem.at[groups[d], tile],
            device_id=(groups[d], row_dev), device_id_type=MESH,
        )

    def halo_copy(down, run, tile):
        h, first, count = run
        g = first // ep_local
        e = first - g * ep_local
        at = first - classes[h][0]
        rows = pl.ds(row_count - h, h) if down else pl.ds(0, h)
        return pltpu.make_async_remote_copy(
            src_ref=pieces.at[g, tile, pl.ds(e, count), :, rows, :],
            dst_ref=(above if down else below)[h].at[tile, pl.ds(at, count)],
            send_sem=(down_send if down else up_send).at[class_at[h]],
            recv_sem=(down_recv if down else up_recv).at[run_at[run], tile],
            device_id=(me, row_dev + 1 if down else row_dev - 1), device_id_type=MESH,
        )

    def forward(d, tile):
        for g in range(n):
            @pl.when(groups[d] == g)
            def _():
                @pl.when(has_below)
                def _():
                    for run in runs[g]:
                        halo_copy(True, run, tile).start()

                @pl.when(has_above)
                def _():
                    for run in runs[g]:
                        halo_copy(False, run, tile).start()

    def wait_halo(g, tile):
        @pl.when(has_above)
        def _():
            for run in runs[g]:
                halo_copy(True, run, tile).wait_recv()

        @pl.when(has_below)
        def _():
            for run in runs[g]:
                halo_copy(False, run, tile).wait_recv()

    def clear_edges():
        for edge, refs in ((has_above, above), (has_below, below)):
            @pl.when(jnp.logical_not(edge))
            def _():
                for h, ref in refs.items():
                    for tile in range(tiles):
                        ref[tile] = jnp.zeros(ref.shape[1:], ref.dtype)

    first_row = jnp.where(has_above, -row_count, 0)
    end_row = jnp.where(has_below, 2 * row_count, row_count)

    def in_sky(row, size=BSUB):
        rows = lax.broadcasted_iota(jnp.int32, (size, LANES), 0) + row
        return jnp.logical_and(rows >= first_row, rows < end_row)

    def shift_of(level, index):
        number = shift_num[level, index]
        big = 2 * VMAX * 2**LEVELS
        whole = lax.div(number + DEN * big, DEN) - big
        left = number - whole * DEN
        fraction = left.astype(jnp.float32) / DEN
        return whole, whole + jnp.where(left > 0, 1, 0), fraction

    kinds = {}
    for blocks, _ in plans:
        for e, t, lane0, row0, size in blocks:
            key = (row0 - lane0, lane0 if lane0 else 0, bool(lane0))
            kinds.setdefault(key, len(kinds))

    def make_toeplitz():
        w = [psf_rows[b] for b in range(2 * reach + 1)]
        squares = [s * s for s in w]
        column = lax.broadcasted_iota(jnp.int32, (BSUB, LANES), 1)
        line = lax.broadcasted_iota(jnp.int32, (BSUB, LANES), 0)

        def body(b, carry):
            row = b * BSUB - row_count
            to = pl.multiple_of(b * BSUB, BSUB)
            keep = in_sky(row)
            for (offset, lane0, extra), at in kinds.items():
                tap = column - line - row + (offset + reach)
                ok = jnp.logical_and(keep, column >= lane0) if extra else keep
                tap = jnp.where(ok, tap, -1)
                for m, weights in enumerate((w, squares)):
                    value = jnp.zeros((BSUB, LANES), jnp.float32)
                    for a, weight in enumerate(weights):
                        value = jnp.where(tap == a, weight, value)
                    toeplitz[m, at, pl.ds(to, BSUB), :] = value
            return carry

        lax.fori_loop(0, 3 * row_count // BSUB, body, 0)

    def pad_of(g):
        return round_up(VMAX * g * ep_local, SUB)

    def mix(load, at, shift):
        near, far, fraction = shift
        return (1.0 - fraction) * load(at - near) + fraction * load(at - far)

    def make_matrix(g):
        base = g * ep_local
        blocks, used = plans[g]
        depth = len(used) * LANES

        def plane(ref, index):
            return lambda m: lambda at: ref[m, index, pl.ds(at, BSUB), :]

        state = []
        for e in range(ep_local):
            mine = {}
            for b, (epoch, t, lane0, row0, size) in enumerate(blocks):
                if epoch == e:
                    kind = kinds[(row0 - lane0, lane0, bool(lane0))]
                    mine[b] = (("toeplitz", kind), plane(toeplitz, kind))
            state.append(mine)
        planes = 0
        for level in range(local_levels - 1):
            half = 2**level
            made, following = [], [None] * ep_local
            for j in range(ep_local):
                if j & half:
                    continue
                for i in (j, j + half):
                    following[i] = dict(state[j])
                    for b, (_, source) in state[j + half].items():
                        made.append((planes, source, shift_of(level, base + i)))
                        following[i][b] = (("mid", planes), plane(mid, planes))
                        planes += 1
            pad = max(
                round_up(VMAX * (base + (j - j % (2 * half))), SUB) for j in range(ep_local)
            )

            def body(b, carry):
                row = b * BSUB - pad
                at = pl.multiple_of(row_count + row, SUB)
                keep = in_sky(row)
                for to, source, shift in made:
                    for m in range(2):
                        value = mix(source(m), at, shift)
                        mid[m, to, pl.ds(at, BSUB), :] = jnp.where(keep, value, 0.0)
                return carry

            lax.fori_loop(0, (row_count + 2 * pad) // BSUB, body, 0)
            state = following

        level = local_levels - 1
        half = 2**level
        pad = pad_of(g)
        size = row_count + 2 * pad
        entries = {}
        for j in range(half):
            for i in (j, j + half):
                for t in range(len(used)):
                    key = tuple(
                        (b, name, None) for b, (name, _) in state[j].items() if blocks[b][1] == t
                    ) + tuple(
                        (b, name, i) for b, (name, _) in state[j + half].items() if blocks[b][1] == t
                    )
                    entries.setdefault((t, key), []).append(i)
        sources = {name: source for mine in state for name, source in mine.values()}
        shifts = [shift_of(level, base + i) for i in range(ep_local)]
        ref = matrices[g]

        def body(b, carry):
            row = b * BSUB - pad
            at = pl.multiple_of(row_count + row, SUB)
            keep = in_sky(row)
            for (t, key), places in entries.items():
                for m in range(2):
                    value = None
                    for _, name, i in key:
                        load = sources[name](m)
                        part = load(at) if i is None else mix(load, at, shifts[i])
                        if i is not None:
                            part = jnp.where(keep, part, 0.0)
                        value = part if value is None else value + part
                    high = value.astype(jnp.bfloat16)
                    low = (value - high.astype(jnp.float32)).astype(jnp.bfloat16)
                    for i in places:
                        to = pl.multiple_of(i * size + b * BSUB, BSUB)
                        ref[m, pl.ds(to, BSUB), t * LANES:(t + 1) * LANES] = high
                        ref[m, pl.ds(to, BSUB), depth + t * LANES:depth + (t + 1) * LANES] = low
            return carry

        lax.fori_loop(0, size // BSUB, body, 0)

    def gather_rows(g, tile, m):
        blocks, used = plans[g]
        parts = []
        for t, filled in enumerate(used):
            for e, at, lane0, row0, size in sorted(blocks, key=lambda b: b[2]):
                if at != t:
                    continue
                epoch = g * ep_local + e
                h = halo_of(epoch)
                index = epoch - classes[h][0]
                row, end = row0, row0 + size
                if row < 0:
                    parts.append(above[h][tile, index, m, row + h:min(end, 0) + h, :])
                    row = min(end, 0)
                if row < min(end, row_count):
                    parts.append(pieces[g, tile, e, m, row:min(end, row_count), :])
                    row = min(end, row_count)
                if row < end:
                    parts.append(below[h][tile, index, m, row - row_count:end - row_count, :])
            if filled < LANES:
                parts.append(jnp.zeros((LANES - filled, LANES), jnp.bfloat16))
        return jnp.concatenate(parts, axis=0)

    def stack_group(g, tile):
        pad = pad_of(g)
        size = row_count + 2 * pad
        for m in range(2):
            x = gather_rows(g, tile, m)
            x = jnp.concatenate([x, x], axis=0)
            y = jnp.dot(matrices[g][m], x, preferred_element_type=jnp.float32)
            for i in range(ep_local):
                wide[0][g * ep_local + i, m, row_count - pad:row_count + row_count + pad, :] = (
                    y[i * size:(i + 1) * size]
                )

    keep_above = jnp.where(has_above, 1.0, 0.0).astype(jnp.float32)
    keep_below = jnp.where(has_below, 1.0, 0.0).astype(jnp.float32)

    def level_pass(level, src, dest, first):
        half = 2**level
        pad = round_up(VMAX * first, SUB)
        for j in range(first, first + half):
            outs = [(i, shift_of(level, i)) for i in (j, j + half)]
            for row in range(-pad, row_count + pad, SUB):
                at = row_count + row
                for m in range(2):
                    lower = src[j, m, at:at + SUB, :]
                    for i, (near, far, fraction) in outs:
                        x = src[j + half, m, pl.ds(at - near, SUB), :]
                        y = src[j + half, m, pl.ds(at - far, SUB), :]
                        value = lower + ((1.0 - fraction) * x + fraction * y)
                        if row < 0:
                            value = value * keep_above
                        if row >= row_count:
                            value = value * keep_below
                        dest[i, m, at:at + SUB, :] = value

    def finish(tile):
        for level in range(local_levels, LEVELS - 1):
            for first in range(0, epochs, 2 ** (level + 1)):
                level_pass(level, wide[level - local_levels], wide[level - local_levels + 1], first)
        final = wide[LEVELS - 1 - local_levels]
        half = epochs // 2
        shifts = [shift_of(LEVELS - 1, i) for i in range(epochs)]

        def body(b, carry):
            at = pl.multiple_of(row_count + b * SUB, SUB)
            likelihood = [None] * epochs
            for j in range(half):
                lower = [final[j, m, pl.ds(at, SUB), :] for m in range(2)]
                for index in (j, j + half):
                    near, far, fraction = shifts[index]
                    maps = []
                    for m in range(2):
                        x = final[j + half, m, pl.ds(at - near, SUB), :]
                        y = final[j + half, m, pl.ds(at - far, SUB), :]
                        maps.append(lower[m] + ((1.0 - fraction) * x + fraction * y))
                    likelihood[index] = maps[0] * lax.rsqrt(maps[1])
            peak = functools.reduce(jnp.maximum, likelihood)
            total = functools.reduce(jnp.add, [jnp.exp(x - peak) for x in likelihood])
            to = pl.multiple_of(b * SUB, SUB)
            out[pl.ds(to, SUB), tile * LANES:(tile + 1) * LANES] = peak + jnp.log(total)
            return carry

        lax.fori_loop(0, row_count // SUB, body, 0)

    make_bands()
    for load in loads:
        load.wait()
    order = send_order(n)
    for tile in range(tiles):
        for d in order:
            filter_cols(groups[d], tile, outgoing.at[d - 1, tile] if d else pieces.at[me, tile])
            if tile == 0 and d == order[0]:
                near = jnp.where(has_above, 1, 0) + jnp.where(has_below, 1, 0)
                pl.semaphore_wait(barrier, n - 1 + near)
            if d:
                piece_out(d, tile).start()
            else:
                forward(0, tile)

    clear_edges()
    make_toeplitz()
    for g in range(n):
        make_matrix(g)

    def process(tile):
        for g in range(n):
            wait_halo(g, tile)
            stack_group(g, tile)
        finish(tile)

    for tile in range(tiles):
        for d in order:
            if d:
                piece_in(d, tile).wait_recv()
                forward(d, tile)
        if tile:
            process(tile - 1)
    process(tiles - 1)

    pltpu.make_async_remote_copy(
        src_ref=outgoing, dst_ref=pieces.at[pl.ds(0, n - 1)], send_sem=send_sem.at[0],
        recv_sem=recv_sem.at[0, 0], device_id=(groups[1], row_dev), device_id_type=MESH,
    ).wait_send()
    for edge, refs, sem, step in ((has_below, above, down_send, 1), (has_above, below, up_send, -1)):
        @pl.when(edge)
        def _():
            for h, ref in refs.items():
                pltpu.make_async_remote_copy(
                    src_ref=ref, dst_ref=ref, send_sem=sem.at[class_at[h]],
                    recv_sem=down_recv.at[0, 0], device_id=(me, row_dev + step),
                    device_id_type=MESH,
                ).wait_send()


def on_device(n, sky, image, inv_variance, psf_rows, psf_cols, shift_num):
    ep_local, row_count, cols = image.shape
    tiles = cols // n // LANES
    epochs = n * ep_local
    local_levels = ep_local.bit_length() - 1
    piece = (tiles, ep_local, 2, row_count, LANES)
    classes = classes_of(epochs)
    plans = [plan_of(g, ep_local, row_count) for g in range(n)]
    kinds = {(b[3] - b[2], b[2]) for blocks, _ in plans for b in blocks}
    run_count = sum(len(runs_of(g, ep_local)) for g in range(n))
    halos = [
        pltpu.VMEM((tiles, count, 2, h, LANES), jnp.bfloat16) for h, (_, count) in classes.items()
    ]
    matrices = []
    for g in range(n):
        size = row_count + 2 * round_up(VMAX * g * ep_local, SUB)
        depth = 2 * LANES * len(plans[g][1])
        matrices.append(pltpu.VMEM((2, ep_local * size, depth), jnp.bfloat16))
    most = max(len(blocks) for blocks, _ in plans)

    any_space = pl.BlockSpec(memory_space=pl.ANY)
    vmem = pl.BlockSpec(memory_space=pltpu.VMEM)
    smem = pl.BlockSpec(memory_space=pltpu.SMEM)
    return pl.pallas_call(
        functools.partial(kernel, n, sky),
        out_shape=jax.ShapeDtypeStruct((row_count, cols // n), jnp.float32),
        in_specs=[any_space, any_space, smem, smem, smem],
        out_specs=vmem,
        scratch_shapes=[
            pltpu.VMEM(image.shape, jnp.bfloat16),
            pltpu.VMEM(image.shape, jnp.bfloat16),
            pltpu.VMEM((n - 1,) + piece, jnp.bfloat16),
            pltpu.VMEM((n,) + piece, jnp.bfloat16),
            pltpu.VMEM((2, 2 * LANES, 2 * LANES), jnp.bfloat16),
            pltpu.VMEM((2, len(kinds), 3 * row_count, LANES), jnp.float32),
            pltpu.VMEM((2, max(1, local_levels * most), 3 * row_count, LANES), jnp.float32),
        ]
        + halos + halos + matrices
        + [
            pltpu.VMEM((epochs, 2, 3 * row_count, LANES), jnp.float32)
            for _ in range(LEVELS - local_levels)
        ]
        + [
            pltpu.SemaphoreType.DMA((2,)),
            pltpu.SemaphoreType.DMA((1,)),
            pltpu.SemaphoreType.DMA((n, tiles)),
            pltpu.SemaphoreType.DMA((len(classes),)),
            pltpu.SemaphoreType.DMA((run_count, tiles)),
            pltpu.SemaphoreType.DMA((len(classes),)),
            pltpu.SemaphoreType.DMA((run_count, tiles)),
        ],
        compiler_params=pltpu.CompilerParams(
            collective_id=0, has_side_effects=True, vmem_limit_bytes=60 * 1024 * 1024
        ),
    )(image, inv_variance, psf_rows, psf_cols, shift_num)


def solution(mesh):
    body = functools.partial(on_device, mesh.shape["epoch"], mesh.shape["sky"])
    return jax.shard_map(
        body,
        mesh=mesh,
        in_specs=(P("epoch", "sky", None), P("epoch", "sky", None), P(), P(), P()),
        out_specs=P("sky", "epoch"),
        check_vma=False,
    )
```

time: 37 us -> 32.4 us (0.88)
  Pallas kernels: 35.3 us -> 30.6 us
    pallas_call x1, Pallas kernels: 35.3 us -> 30.6 us  [on_device(): pl.pallas_call(functools.partial(kernel, n, sky), out_shape=jax.ShapeDtyp...]
where the time goes in v1:
time: 32.4 us; the launch traced here: 32.2 us
  Pallas kernels  30.6 us (94%)
  local copies, waits for them, and re-layouts  1.54 us (5%)
    pallas_call x1, Pallas kernels, on_device(): pl.pallas_call(functools.partial(kernel, n, sky), out_shape=jax.ShapeDtyp...  30.6 us
    unnamed x1, local copies, waits for them, and re-layouts  1.54 us

profile of v1, /device:TPU:1, one launch (start us, length us, event | category | flops | bytes accessed | tf_op | source)
XLA Modules:
  0.0 32.2 jit_solution(8730350993427589669)
XLA Ops:
  0.0 30.6 %shard_map.55 = f32[48,512]{1,0:T(8,128)} custom-call(bf16[4,48,2048]{2,1,0:T(8,128)(2,1)} %image_hbm.1, bf16[4,48,2048]{2,1,0:T(8,128)(2,1)} %variance_hbm.1, f32[9]{0:T(128)} %psf_rows.1, f32[9]{0:T(128)} %psf_cols.1, s32[4,16]{1,0:T(4,128)} %shift_num.1), custom_call_target="tpu_custom_call" | custom-call | tf_op jit(solution)/shard_map/pallas_call | solution.py:538
  30.6 1.5 %copy.7 = f32[48,512]{1,0:T(8,128)} copy(f32[48,512]{1,0:T(8,128)} %shard_map.55) | data formatting | bytes 196608

commit v2 on v1

--- a/solution.py
+++ b/solution.py
@@ -42,9 +42,9 @@
     return found
 
 
-def runs_of(g, ep_local):
+def runs_of(start, count):
     runs = []
-    for e in range(g * ep_local, (g + 1) * ep_local):
+    for e in range(start, start + count):
         if runs and runs[-1][0] == halo_of(e):
             runs[-1] = (runs[-1][0], runs[-1][1], runs[-1][2] + 1)
         else:
@@ -72,18 +72,21 @@
     return blocks, used
 
 
-SEND_ORDER = "3120"
-
-
 def send_order(n):
-    if n == len(SEND_ORDER):
-        return [int(c) for c in SEND_ORDER]
-    return list(range(n - 1, 0, -1)) + [0]
+    return sorted(range(1, n), key=lambda d: (-bin(d).count("1"), d)) + [0]
+
+
+def parts_of(tile, tiles, ep_local):
+    if tile < tiles - 1 or ep_local == 1:
+        return [(0, ep_local, tile)]
+    half = ep_local // 2
+    return [(0, half, tile), (half, ep_local - half, tiles)]
 
 
 def kernel(
-    n, sky, image_hbm, variance_hbm, psf_rows, psf_cols, shift_num, out,
-    image, variance, outgoing, pieces, bands, toeplitz, mid, *rest,
+    n, sky, image_hbm, variance_hbm, psf_rows_hbm, psf_cols_hbm, shift_hbm, out,
+    image, variance, psf_rows, psf_cols, shift_num,
+    outgoing, pieces, bands, toeplitz, mid, counted, *rest,
 ):
     ep_local, row_count = image.shape[0], image.shape[1]
     epochs = n * ep_local
@@ -91,19 +94,13 @@
     reach = PSF_HALF
     local_levels = ep_local.bit_length() - 1
     classes = classes_of(epochs)
-    runs = [runs_of(g, ep_local) for g in range(n)]
     plans = [plan_of(g, ep_local, row_count) for g in range(n)]
     rest = list(rest)
     above = {h: rest.pop(0) for h in classes}
     below = {h: rest.pop(0) for h in classes}
     matrices = [rest.pop(0) for _ in range(n)]
     wide = [rest.pop(0) for _ in range(LEVELS - local_levels)]
-    in_sem, send_sem, recv_sem, down_send, down_recv, up_send, up_recv = rest
-    class_at = {h: i for i, h in enumerate(classes)}
-    run_at = {}
-    for g in range(n):
-        for run in runs[g]:
-            run_at[run] = len(run_at)
+    in_sem, send_sem, recv_sem, halo_recv = rest
 
     me = lax.axis_index("epoch")
     row_dev = lax.axis_index("sky")
@@ -111,13 +108,6 @@
     has_below = row_dev < sky - 1
     groups = [flip(me, d, n) for d in range(n)]
 
-    loads = [
-        pltpu.make_async_copy(image_hbm, image, in_sem.at[0]),
-        pltpu.make_async_copy(variance_hbm, variance, in_sem.at[1]),
-    ]
-    for load in loads:
-        load.start()
-
     barrier = pltpu.get_barrier_semaphore()
     for d in range(1, n):
         pl.semaphore_signal(barrier, inc=1, device_id=(groups[d], row_dev), device_id_type=MESH)
@@ -129,6 +119,14 @@
     @pl.when(has_below)
     def _():
         pl.semaphore_signal(barrier, inc=1, device_id=(me, row_dev + 1), device_id_type=MESH)
+
+    whole = (
+        (psf_cols_hbm, psf_cols), (image_hbm, image), (variance_hbm, variance),
+        (psf_rows_hbm, psf_rows), (shift_hbm, shift_num),
+    )
+    loads = [pltpu.make_async_copy(a, b, in_sem.at[i]) for i, (a, b) in enumerate(whole)]
+    for load in loads:
+        load.start()
 
     def make_bands():
         source = lax.broadcasted_iota(jnp.int32, (2 * LANES, LANES), 0)
@@ -177,58 +175,67 @@
                 y = y + jnp.dot(low, bands[m, :, :LANES], preferred_element_type=jnp.float32)
             dest[:, m] = y.reshape(ep_local, row_count, LANES).astype(jnp.bfloat16)
 
-    def piece_out(d, tile):
+    def piece_copy(d, tile, part, group):
+        first, count, slot = part
+        epochs_of = pl.ds(first, count)
         return pltpu.make_async_remote_copy(
-            src_ref=outgoing.at[d - 1, tile], dst_ref=pieces.at[me, tile],
-            send_sem=send_sem.at[0], recv_sem=recv_sem.at[me, tile],
+            src_ref=outgoing.at[d - 1, tile, epochs_of], dst_ref=pieces.at[group, tile, epochs_of],
+            send_sem=send_sem.at[0], recv_sem=recv_sem.at[d - 1, slot],
             device_id=(groups[d], row_dev), device_id_type=MESH,
         )
 
-    def piece_in(d, tile):
-        return pltpu.make_async_remote_copy(
-            src_ref=outgoing.at[d - 1, tile], dst_ref=pieces.at[groups[d], tile],
-            send_sem=send_sem.at[0], recv_sem=recv_sem.at[groups[d], tile],
-            device_id=(groups[d], row_dev), device_id_type=MESH,
-        )
-
-    def halo_copy(down, run, tile):
-        h, first, count = run
-        g = first // ep_local
-        e = first - g * ep_local
-        at = first - classes[h][0]
+    def halo_copy(down, run, tile, slot):
+        h, start, count = run
+        g = start // ep_local
+        at = start - classes[h][0]
         rows = pl.ds(row_count - h, h) if down else pl.ds(0, h)
         return pltpu.make_async_remote_copy(
-            src_ref=pieces.at[g, tile, pl.ds(e, count), :, rows, :],
+            src_ref=pieces.at[g, tile, pl.ds(start - g * ep_local, count), :, rows, :],
             dst_ref=(above if down else below)[h].at[tile, pl.ds(at, count)],
-            send_sem=(down_send if down else up_send).at[class_at[h]],
-            recv_sem=(down_recv if down else up_recv).at[run_at[run], tile],
+            send_sem=send_sem.at[1 if down else 2], recv_sem=halo_recv.at[g, slot],
             device_id=(me, row_dev + 1 if down else row_dev - 1), device_id_type=MESH,
         )
 
-    def forward(d, tile):
+    def each_group(d, use):
         for g in range(n):
-            @pl.when(groups[d] == g)
+            pl.when(groups[d] == g)(functools.partial(use, g))
+
+    def forward(d, tile, part):
+        first, count, slot = part
+
+        def use(g):
+            runs = runs_of(g * ep_local + first, count)
+
+            @pl.when(has_below)
             def _():
-                @pl.when(has_below)
-                def _():
-                    for run in runs[g]:
-                        halo_copy(True, run, tile).start()
-
-                @pl.when(has_above)
-                def _():
-                    for run in runs[g]:
-                        halo_copy(False, run, tile).start()
-
-    def wait_halo(g, tile):
-        @pl.when(has_above)
+                for run in runs:
+                    halo_copy(True, run, tile, slot).start()
+
+            @pl.when(has_above)
+            def _():
+                for run in runs:
+                    halo_copy(False, run, tile, slot).start()
+
+        each_group(d, use)
+
+    def counting(rows, send, recv):
+        return pltpu.make_async_remote_copy(
+            src_ref=counted.at[pl.ds(0, rows)], dst_ref=counted.at[pl.ds(0, rows)],
+            send_sem=send, recv_sem=recv, device_id=(groups[1], row_dev), device_id_type=MESH,
+        )
+
+    def wait_halo(g, part):
+        first, count, slot = part
+        rows = sum(2 * h * c for h, _, c in runs_of(g * ep_local + first, count))
+        sem = halo_recv.at[g, slot]
+
+        @pl.when(jnp.logical_and(has_above, has_below))
         def _():
-            for run in runs[g]:
-                halo_copy(True, run, tile).wait_recv()
-
-        @pl.when(has_below)
+            counting(2 * rows, send_sem.at[0], sem).wait_recv()
+
+        @pl.when(has_above != has_below)
         def _():
-            for run in runs[g]:
-                halo_copy(False, run, tile).wait_recv()
+            counting(rows, send_sem.at[0], sem).wait_recv()
 
     def clear_edges():
         for edge, refs in ((has_above, above), (has_below, below)):
@@ -419,13 +426,14 @@
         pad = round_up(VMAX * first, SUB)
         for j in range(first, first + half):
             outs = [(i, shift_of(level, i)) for i in (j, j + half)]
+            outs = [(i, row_count - near, row_count - far, f) for i, (near, far, f) in outs]
             for row in range(-pad, row_count + pad, SUB):
                 at = row_count + row
                 for m in range(2):
                     lower = src[j, m, at:at + SUB, :]
-                    for i, (near, far, fraction) in outs:
-                        x = src[j + half, m, pl.ds(at - near, SUB), :]
-                        y = src[j + half, m, pl.ds(at - far, SUB), :]
+                    for i, near, far, fraction in outs:
+                        x = src[j + half, m, pl.ds(near + row, SUB), :]
+                        y = src[j + half, m, pl.ds(far + row, SUB), :]
                         value = lower + ((1.0 - fraction) * x + fraction * y)
                         if row < 0:
                             value = value * keep_above
@@ -440,30 +448,28 @@
         final = wide[LEVELS - 1 - local_levels]
         half = epochs // 2
         shifts = [shift_of(LEVELS - 1, i) for i in range(epochs)]
-
-        def body(b, carry):
-            at = pl.multiple_of(row_count + b * SUB, SUB)
+        shifts = [(row_count - near, row_count - far, f) for near, far, f in shifts]
+
+        for row in range(0, row_count, SUB):
+            at = row_count + row
             likelihood = [None] * epochs
             for j in range(half):
-                lower = [final[j, m, pl.ds(at, SUB), :] for m in range(2)]
+                lower = [final[j, m, at:at + SUB, :] for m in range(2)]
                 for index in (j, j + half):
                     near, far, fraction = shifts[index]
                     maps = []
                     for m in range(2):
-                        x = final[j + half, m, pl.ds(at - near, SUB), :]
-                        y = final[j + half, m, pl.ds(at - far, SUB), :]
+                        x = final[j + half, m, pl.ds(near + row, SUB), :]
+                        y = final[j + half, m, pl.ds(far + row, SUB), :]
                         maps.append(lower[m] + ((1.0 - fraction) * x + fraction * y))
                     likelihood[index] = maps[0] * lax.rsqrt(maps[1])
             peak = functools.reduce(jnp.maximum, likelihood)
             total = functools.reduce(jnp.add, [jnp.exp(x - peak) for x in likelihood])
-            to = pl.multiple_of(b * SUB, SUB)
-            out[pl.ds(to, SUB), tile * LANES:(tile + 1) * LANES] = peak + jnp.log(total)
-            return carry
-
-        lax.fori_loop(0, row_count // SUB, body, 0)
-
+            out[row:row + SUB, tile * LANES:(tile + 1) * LANES] = peak + jnp.log(total)
+
+    loads[0].wait()
     make_bands()
-    for load in loads:
+    for load in loads[1:]:
         load.wait()
     order = send_order(n)
     for tile in range(tiles):
@@ -472,44 +478,47 @@
             if tile == 0 and d == order[0]:
                 near = jnp.where(has_above, 1, 0) + jnp.where(has_below, 1, 0)
                 pl.semaphore_wait(barrier, n - 1 + near)
+            parts = parts_of(tile, tiles, ep_local)
             if d:
-                piece_out(d, tile).start()
+                piece_copy(d, tile, parts[0], me).start()
             else:
-                forward(0, tile)
+                for part in parts[1:]:
+                    for other in order[:-1]:
+                        piece_copy(other, tile, part, me).start()
+                for part in parts:
+                    forward(0, tile, part)
 
     clear_edges()
     make_toeplitz()
     for g in range(n):
         make_matrix(g)
 
-    def process(tile):
-        for g in range(n):
-            wait_halo(g, tile)
-            stack_group(g, tile)
-        finish(tile)
+    def stack_tile(g, tile):
+        for part in parts_of(tile, tiles, ep_local):
+            wait_halo(g, part)
+        stack_group(g, tile)
 
     for tile in range(tiles):
-        for d in order:
-            if d:
-                piece_in(d, tile).wait_recv()
-                forward(d, tile)
+        for part in parts_of(tile, tiles, ep_local):
+            for d in order[:-1]:
+                piece_copy(d, tile, part, groups[d]).wait_recv()
+                forward(d, tile, part)
         if tile:
-            process(tile - 1)
-    process(tiles - 1)
+            for g in range(n):
+                stack_tile(g, tile - 1)
+            finish(tile - 1)
+    for d in [0] + order[:-1]:
+        each_group(d, functools.partial(stack_tile, tile=tiles - 1))
+    finish(tiles - 1)
 
     pltpu.make_async_remote_copy(
         src_ref=outgoing, dst_ref=pieces.at[pl.ds(0, n - 1)], send_sem=send_sem.at[0],
         recv_sem=recv_sem.at[0, 0], device_id=(groups[1], row_dev), device_id_type=MESH,
     ).wait_send()
-    for edge, refs, sem, step in ((has_below, above, down_send, 1), (has_above, below, up_send, -1)):
+    for edge, sem in ((has_below, send_sem.at[1]), (has_above, send_sem.at[2])):
         @pl.when(edge)
         def _():
-            for h, ref in refs.items():
-                pltpu.make_async_remote_copy(
-                    src_ref=ref, dst_ref=ref, send_sem=sem.at[class_at[h]],
-                    recv_sem=down_recv.at[0, 0], device_id=(me, row_dev + step),
-                    device_id_type=MESH,
-                ).wait_send()
+            counting(counted.shape[0], sem, recv_sem.at[0, 0]).wait_send()
 
 
 def on_device(n, sky, image, inv_variance, psf_rows, psf_cols, shift_num):
@@ -521,7 +530,7 @@
     classes = classes_of(epochs)
     plans = [plan_of(g, ep_local, row_count) for g in range(n)]
     kinds = {(b[3] - b[2], b[2]) for blocks, _ in plans for b in blocks}
-    run_count = sum(len(runs_of(g, ep_local)) for g in range(n))
+    halo_rows = sum(2 * tiles * halo_of(e) for e in range(epochs))
     halos = [
         pltpu.VMEM((tiles, count, 2, h, LANES), jnp.bfloat16) for h, (_, count) in classes.items()
     ]
@@ -534,20 +543,23 @@
 
     any_space = pl.BlockSpec(memory_space=pl.ANY)
     vmem = pl.BlockSpec(memory_space=pltpu.VMEM)
-    smem = pl.BlockSpec(memory_space=pltpu.SMEM)
     return pl.pallas_call(
         functools.partial(kernel, n, sky),
-        out_shape=jax.ShapeDtypeStruct((row_count, cols // n), jnp.float32),
-        in_specs=[any_space, any_space, smem, smem, smem],
+        out_shape=pltpu.VMEM((row_count, cols // n), jnp.float32),
+        in_specs=[any_space] * 5,
         out_specs=vmem,
         scratch_shapes=[
             pltpu.VMEM(image.shape, jnp.bfloat16),
             pltpu.VMEM(image.shape, jnp.bfloat16),
+            pltpu.SMEM(psf_rows.shape, jnp.float32),
+            pltpu.SMEM(psf_cols.shape, jnp.float32),
+            pltpu.SMEM(shift_num.shape, jnp.int32),
             pltpu.VMEM((n - 1,) + piece, jnp.bfloat16),
             pltpu.VMEM((n,) + piece, jnp.bfloat16),
             pltpu.VMEM((2, 2 * LANES, 2 * LANES), jnp.bfloat16),
             pltpu.VMEM((2, len(kinds), 3 * row_count, LANES), jnp.float32),
             pltpu.VMEM((2, max(1, local_levels * most), 3 * row_count, LANES), jnp.float32),
+            pltpu.VMEM((halo_rows, LANES), jnp.bfloat16),
         ]
         + halos + halos + matrices
         + [
@@ -555,13 +567,10 @@
             for _ in range(LEVELS - local_levels)
         ]
         + [
-            pltpu.SemaphoreType.DMA((2,)),
-            pltpu.SemaphoreType.DMA((1,)),
-            pltpu.SemaphoreType.DMA((n, tiles)),
-            pltpu.SemaphoreType.DMA((len(classes),)),
-            pltpu.SemaphoreType.DMA((run_count, tiles)),
-            pltpu.SemaphoreType.DMA((len(classes),)),
-            pltpu.SemaphoreType.DMA((run_count, tiles)),
+            pltpu.SemaphoreType.DMA((5,)),
+            pltpu.SemaphoreType.DMA((3,)),
+            pltpu.SemaphoreType.DMA((n - 1, tiles + 1)),
+            pltpu.SemaphoreType.DMA((n, tiles + 1)),
         ],
         compiler_params=pltpu.CompilerParams(
             collective_id=0, has_side_effects=True, vmem_limit_bytes=60 * 1024 * 1024

time: 32.4 us -> 29.2 us (0.901)
  Pallas kernels: 30.6 us -> 28.4 us
  local copies, waits for them, and re-layouts: 1.54 us -> 0.64 us
    pallas_call x1, Pallas kernels: 30.6 us -> 28.4 us  [on_device(): pl.pallas_call(functools.partial(kernel, n, sky), out_shape=pltpu.VMEM((r...]
    unnamed x1, local copies, waits for them, and re-layouts: 1.54 us -> 0.64 us
where the time goes in v2:
time: 29.2 us; the launch traced here: 29.1 us
  Pallas kernels  28.4 us (97%)
  local copies, waits for them, and re-layouts  0.64 us (2%)
    pallas_call x1, Pallas kernels, on_device(): pl.pallas_call(functools.partial(kernel, n, sky), out_shape=pltpu.VMEM((r...  28.4 us
    unnamed x1, local copies, waits for them, and re-layouts  0.64 us

profile of v2, /device:TPU:1, one launch (start us, length us, event | category | flops | bytes accessed | tf_op | source)
XLA Modules:
  0.0 29.1 jit_solution(7799631447446233487)
XLA Ops:
  0.0 28.4 %shard_map.55 = f32[48,512]{1,0:T(8,128)S(1)} custom-call(bf16[4,48,2048]{2,1,0:T(8,128)(2,1)} %image_hbm.1, bf16[4,48,2048]{2,1,0:T(8,128)(2,1)} %variance_hbm.1, f32[9]{0:T(128)} %psf_rows_hbm.1, f32[9]{0:T(128)} %psf_cols_hbm.1, s32[4,16]{1,0:T(4,128)} %shift_hbm.1), custom_call_target="tpu_custom_call" | custom-call | tf_op jit(solution)/shard_map/pallas_call | solution.py:546
  28.4 0.6 %copy.7 = f32[48,512]{1,0:T(8,128)} copy(f32[48,512]{1,0:T(8,128)S(1)} %shard_map.55) | data formatting | bytes 196608

commit v3 on v2

--- a/solution.py
+++ b/solution.py
@@ -14,6 +14,8 @@
 LANES = 128
 SUB = 8
 BSUB = 16
+FINAL = 16
+HOLD = 1
 MESH = pl.DeviceIdType.MESH
 
 
@@ -418,28 +420,21 @@
                     y[i * size:(i + 1) * size]
                 )
 
-    keep_above = jnp.where(has_above, 1.0, 0.0).astype(jnp.float32)
-    keep_below = jnp.where(has_below, 1.0, 0.0).astype(jnp.float32)
-
     def level_pass(level, src, dest, first):
         half = 2**level
         pad = round_up(VMAX * first, SUB)
+        start, size = row_count - pad, row_count + 2 * pad
+        if pad:
+            lines = lax.broadcasted_iota(jnp.int32, (size, LANES), 0) - pad
+            keep = jnp.logical_and(lines >= first_row, lines < end_row)
         for j in range(first, first + half):
-            outs = [(i, shift_of(level, i)) for i in (j, j + half)]
-            outs = [(i, row_count - near, row_count - far, f) for i, (near, far, f) in outs]
-            for row in range(-pad, row_count + pad, SUB):
-                at = row_count + row
+            for i in (j, j + half):
+                near, far, fraction = shift_of(level, i)
                 for m in range(2):
-                    lower = src[j, m, at:at + SUB, :]
-                    for i, near, far, fraction in outs:
-                        x = src[j + half, m, pl.ds(near + row, SUB), :]
-                        y = src[j + half, m, pl.ds(far + row, SUB), :]
-                        value = lower + ((1.0 - fraction) * x + fraction * y)
-                        if row < 0:
-                            value = value * keep_above
-                        if row >= row_count:
-                            value = value * keep_below
-                        dest[i, m, at:at + SUB, :] = value
+                    x = src[j + half, m, pl.ds(start - near, size), :]
+                    y = src[j + half, m, pl.ds(start - far, size), :]
+                    value = src[j, m, start:start + size, :] + ((1.0 - fraction) * x + fraction * y)
+                    dest[i, m, start:start + size, :] = jnp.where(keep, value, 0.0) if pad else value
 
     def finish(tile):
         for level in range(local_levels, LEVELS - 1):
@@ -448,45 +443,58 @@
         final = wide[LEVELS - 1 - local_levels]
         half = epochs // 2
         shifts = [shift_of(LEVELS - 1, i) for i in range(epochs)]
-        shifts = [(row_count - near, row_count - far, f) for near, far, f in shifts]
-
-        for row in range(0, row_count, SUB):
+        for row in range(0, row_count, FINAL):
             at = row_count + row
             likelihood = [None] * epochs
             for j in range(half):
-                lower = [final[j, m, at:at + SUB, :] for m in range(2)]
+                lower = [final[j, m, at:at + FINAL, :] for m in range(2)]
                 for index in (j, j + half):
                     near, far, fraction = shifts[index]
                     maps = []
                     for m in range(2):
-                        x = final[j + half, m, pl.ds(near + row, SUB), :]
-                        y = final[j + half, m, pl.ds(far + row, SUB), :]
+                        x = final[j + half, m, pl.ds(at - near, FINAL), :]
+                        y = final[j + half, m, pl.ds(at - far, FINAL), :]
                         maps.append(lower[m] + ((1.0 - fraction) * x + fraction * y))
                     likelihood[index] = maps[0] * lax.rsqrt(maps[1])
             peak = functools.reduce(jnp.maximum, likelihood)
             total = functools.reduce(jnp.add, [jnp.exp(x - peak) for x in likelihood])
-            out[row:row + SUB, tile * LANES:(tile + 1) * LANES] = peak + jnp.log(total)
+            out[row:row + FINAL, tile * LANES:(tile + 1) * LANES] = peak + jnp.log(total)
 
     loads[0].wait()
     make_bands()
     for load in loads[1:]:
         load.wait()
     order = send_order(n)
+    first_core = lax.rem(row_dev, 2) == 0
     for tile in range(tiles):
         for d in order:
             filter_cols(groups[d], tile, outgoing.at[d - 1, tile] if d else pieces.at[me, tile])
             if tile == 0 and d == order[0]:
                 near = jnp.where(has_above, 1, 0) + jnp.where(has_below, 1, 0)
                 pl.semaphore_wait(barrier, n - 1 + near)
-            parts = parts_of(tile, tiles, ep_local)
             if d:
-                piece_copy(d, tile, parts[0], me).start()
-            else:
-                for part in parts[1:]:
-                    for other in order[:-1]:
-                        piece_copy(other, tile, part, me).start()
-                for part in parts:
-                    forward(0, tile, part)
+                @pl.when(first_core)
+                def _():
+                    piece_copy(d, tile, parts_of(tile, tiles, ep_local)[0], me).start()
+
+        parts = parts_of(tile, tiles, ep_local)
+
+        @pl.when(first_core)
+        def _():
+            for part in parts[1:]:
+                for d in order[:-1]:
+                    piece_copy(d, tile, part, me).start()
+
+        if tile >= HOLD or tile == tiles - 1:
+            @pl.when(jnp.logical_not(first_core))
+            def _():
+                for now in range(tile + 1) if tile == min(HOLD, tiles - 1) else [tile]:
+                    for part in parts_of(now, tiles, ep_local):
+                        for d in order[:-1]:
+                            piece_copy(d, now, part, me).start()
+
+        for part in parts:
+            forward(0, tile, part)
 
     clear_edges()
     make_toeplitz()

time: 29.2 us -> 29 us (level)
  no operation moved by 1% of the time
where the time goes in v3:
time: 29 us; the launch traced here: 28.9 us
  Pallas kernels  28.2 us (97%)
  local copies, waits for them, and re-layouts  0.64 us (2%)
    pallas_call x1, Pallas kernels, on_device(): pl.pallas_call(functools.partial(kernel, n, sky), out_shape=pltpu.VMEM((r...  28.2 us
    unnamed x1, local copies, waits for them, and re-layouts  0.64 us

profile of v3, /device:TPU:1, one launch (start us, length us, event | category | flops | bytes accessed | tf_op | source)
XLA Modules:
  0.0 28.9 jit_solution(6225788407382047373)
XLA Ops:
  0.0 28.2 %shard_map.55 = f32[48,512]{1,0:T(8,128)S(1)} custom-call(bf16[4,48,2048]{2,1,0:T(8,128)(2,1)} %image_hbm.1, bf16[4,48,2048]{2,1,0:T(8,128)(2,1)} %variance_hbm.1, f32[9]{0:T(128)} %psf_rows_hbm.1, f32[9]{0:T(128)} %psf_cols_hbm.1, s32[4,16]{1,0:T(4,128)} %shift_hbm.1), custom_call_target="tpu_custom_call" | custom-call | tf_op jit(solution)/shard_map/pallas_call | solution.py:554
  28.2 0.6 %copy.7 = f32[48,512]{1,0:T(8,128)} copy(f32[48,512]{1,0:T(8,128)S(1)} %shard_map.55) | data formatting | bytes 196608

commit v4 on v3

--- a/solution.py
+++ b/solution.py
@@ -82,7 +82,7 @@
     if tile < tiles - 1 or ep_local == 1:
         return [(0, ep_local, tile)]
     half = ep_local // 2
-    return [(0, half, tile), (half, ep_local - half, tiles)]
+    return [(half, ep_local - half, tile), (0, half, tiles)]
 
 
 def kernel(
@@ -186,6 +186,10 @@
             device_id=(groups[d], row_dev), device_id_type=MESH,
         )
 
+    def halo_sem(g, slot):
+        last = tiles - 1
+        return halo_recv.at[slot if slot < last else last + 2 * g + slot - last]
+
     def halo_copy(down, run, tile, slot):
         h, start, count = run
         g = start // ep_local
@@ -194,7 +198,7 @@
         return pltpu.make_async_remote_copy(
             src_ref=pieces.at[g, tile, pl.ds(start - g * ep_local, count), :, rows, :],
             dst_ref=(above if down else below)[h].at[tile, pl.ds(at, count)],
-            send_sem=send_sem.at[1 if down else 2], recv_sem=halo_recv.at[g, slot],
+            send_sem=send_sem.at[1 if down else 2], recv_sem=halo_sem(g, slot),
             device_id=(me, row_dev + 1 if down else row_dev - 1), device_id_type=MESH,
         )
 
@@ -226,10 +230,10 @@
             send_sem=send, recv_sem=recv, device_id=(groups[1], row_dev), device_id_type=MESH,
         )
 
-    def wait_halo(g, part):
+    def wait_halo(which, part):
         first, count, slot = part
-        rows = sum(2 * h * c for h, _, c in runs_of(g * ep_local + first, count))
-        sem = halo_recv.at[g, slot]
+        rows = sum(2 * h * c for g in which for h, _, c in runs_of(g * ep_local + first, count))
+        sem = halo_sem(which[0], slot)
 
         @pl.when(jnp.logical_and(has_above, has_below))
         def _():
@@ -501,10 +505,10 @@
     for g in range(n):
         make_matrix(g)
 
-    def stack_tile(g, tile):
-        for part in parts_of(tile, tiles, ep_local):
-            wait_halo(g, part)
-        stack_group(g, tile)
+    def stack_last(g):
+        for part in parts_of(tiles - 1, tiles, ep_local):
+            wait_halo([g], part)
+        stack_group(g, tiles - 1)
 
     for tile in range(tiles):
         for part in parts_of(tile, tiles, ep_local):
@@ -512,11 +516,13 @@
                 piece_copy(d, tile, part, groups[d]).wait_recv()
                 forward(d, tile, part)
         if tile:
+            for part in parts_of(tile - 1, tiles, ep_local):
+                wait_halo(range(n), part)
             for g in range(n):
-                stack_tile(g, tile - 1)
+                stack_group(g, tile - 1)
             finish(tile - 1)
     for d in [0] + order[:-1]:
-        each_group(d, functools.partial(stack_tile, tile=tiles - 1))
+        each_group(d, stack_last)
     finish(tiles - 1)
 
     pltpu.make_async_remote_copy(
@@ -578,7 +584,7 @@
             pltpu.SemaphoreType.DMA((5,)),
             pltpu.SemaphoreType.DMA((3,)),
             pltpu.SemaphoreType.DMA((n - 1, tiles + 1)),
-            pltpu.SemaphoreType.DMA((n, tiles + 1)),
+            pltpu.SemaphoreType.DMA((tiles - 1 + 2 * n,)),
         ],
         compiler_params=pltpu.CompilerParams(
             collective_id=0, has_side_effects=True, vmem_limit_bytes=60 * 1024 * 1024

time: 29 us -> 28.4 us (0.979)
  Pallas kernels: 28.2 us -> 27.6 us
    pallas_call x1, Pallas kernels: 28.2 us -> 27.6 us  [on_device(): pl.pallas_call(functools.partial(kernel, n, sky), out_shape=pltpu.VMEM((r...]
where the time goes in v4:
time: 28.4 us; the launch traced here: 28.3 us
  Pallas kernels  27.6 us (97%)
  local copies, waits for them, and re-layouts  0.64 us (2%)
    pallas_call x1, Pallas kernels, on_device(): pl.pallas_call(functools.partial(kernel, n, sky), out_shape=pltpu.VMEM((r...  27.6 us
    unnamed x1, local copies, waits for them, and re-layouts  0.64 us

profile of v4, /device:TPU:1, one launch (start us, length us, event | category | flops | bytes accessed | tf_op | source)
XLA Modules:
  0.0 28.3 jit_solution(1760753341158081743)
XLA Ops:
  0.0 27.6 %shard_map.55 = f32[48,512]{1,0:T(8,128)S(1)} custom-call(bf16[4,48,2048]{2,1,0:T(8,128)(2,1)} %image_hbm.1, bf16[4,48,2048]{2,1,0:T(8,128)(2,1)} %variance_hbm.1, f32[9]{0:T(128)} %psf_rows_hbm.1, f32[9]{0:T(128)} %psf_cols_hbm.1, s32[4,16]{1,0:T(4,128)} %shift_hbm.1), custom_call_target="tpu_custom_call" | custom-call | tf_op jit(solution)/shard_map/pallas_call | solution.py:560
  27.7 0.6 %copy.7 = f32[48,512]{1,0:T(8,128)} copy(f32[48,512]{1,0:T(8,128)S(1)} %shard_map.55) | data formatting | bytes 196608
